TPU v7x, 32 devices: a whole 2x2x4 slice. The times are simulated.
32 devices in a mesh: jpair: 2 (over x), blk: 16 (over z, y, core).
Axes of the slice: x: 2, y: 2, z: 4, core: 2. Of those that a mesh axis runs over, the one named last changes fastest.
Arguments:
- dipole: bfloat16 [256, 12, 3, 256, 256], P('blk'), may hold values from -24 to 24
- block_cols: int32 [256, 12], P('blk'), may hold values from 0 to 255, as said below
- upper_vecs: bfloat16 [131072, 256], P(('jpair', 'blk')), parts along dimension 0, may hold values from -0.0234375 to 0.0234375
- lower_vecs: bfloat16 [131072, 128], P(('jpair', 'blk')), parts along dimension 0, may hold values from -0.0234375 to 0.0234375
- upper_energy: float32 [512], P('jpair'), parts along dimension 0, may hold values from 1 to 2
- lower_energy: float32 [256], P('jpair'), parts along dimension 0, may hold values from 0 to 0.8
Outputs:
- strength: float32 [512, 128], P(('jpair', 'blk')), parts along dimension 0
- intensity: float32 [512, 128], P(('jpair', 'blk')), parts along dimension 0
There are 2 independent parts, one for each index of `jpair`. A program takes and returns all parts, laid end to end along the dimension named above; an argument that names none is the same for every part. Nothing has to cross between parts.
Inputs may be any that keep to these rules, and one draw needn't show every extreme that they name: `block_cols`: within one block row the 12 block columns are distinct, and one of them is the row's own index. Splitting the block rows into 16 equal runs of consecutive rows, the columns of one run that fall in another run number at most 12 distinct blocks for each other run, and exactly 12 for some.
All inputs are finite; a program needn't handle non-finite values.
Results may differ from a plain program's by a relative error of at most 0.0026.
Values may be sent and summed in bfloat16 or wider, within the bound.
A program may use at most 256 MiB of HBM per device.

v0:
```python
import jax
import jax.numpy as jnp
from jax import lax
from jax.sharding import PartitionSpec as P

THERMAL = 0.3


def per_device(dipole, block_cols, upper_vecs, lower_vecs, upper_energy, lower_energy):
    rows_blk, nonzero, n_comps, block_size, _ = dipole.shape
    upper_count = upper_vecs.shape[1]
    lower_count = lower_vecs.shape[1]
    upper_blocks = upper_vecs.reshape(rows_blk, block_size, upper_count)
    halves = jnp.einsum(
        "rkast,rsu->rkatu", dipole, upper_blocks, preferred_element_type=jnp.float32
    ).astype(jnp.bfloat16)
    entry_count = rows_blk * nonzero
    halves = halves.reshape(entry_count, n_comps, block_size, upper_count)
    columns = block_cols.reshape(entry_count)
    group_size = lax.axis_size("blk")
    my_index = lax.axis_index("blk")
    gathered = lax.all_gather(lower_vecs, "blk", axis=0, tiled=True)
    all_blocks = gathered.reshape(gathered.shape[0] // block_size, block_size, lower_count)
    lows = jnp.take(all_blocks, columns, axis=0)
    proj = jnp.einsum("eatu,etl->aul", halves, lows, preferred_element_type=jnp.float32)
    share_rows = upper_count // group_size
    first_row = my_index * share_rows
    summed = lax.psum(proj, "blk")
    own_share = lax.dynamic_slice_in_dim(summed, first_row, share_rows, 1)
    strength = jnp.sum(own_share * own_share, axis=0)
    energy_rows = lax.dynamic_slice_in_dim(upper_energy, first_row, share_rows, 0)
    wavenumber = energy_rows[:, None] - lower_energy[None, :]
    intensity = wavenumber**3 * jnp.exp(-lower_energy / THERMAL)[None, :] * strength
    return (strength, intensity)


def solution(mesh):
    placed = (
        P("blk", None, None, None, None),
        P("blk", None),
        P(("jpair", "blk"), None),
        P(("jpair", "blk"), None),
        P("jpair"),
        P("jpair"),
    )
    return jax.shard_map(
        per_device,
        mesh=mesh,
        in_specs=placed,
        out_specs=(P(("jpair", "blk"), None), P(("jpair", "blk"), None)),
        check_vma=False,
    )
```

profile of v0, /device:TPU:0, one launch (start us, length us, event | category | flops | bytes accessed | tf_op | source)
XLA Modules:
  0.0 283.5 jit_solution(16496702931421474902)
XLA Ops:
  7.2 0.0 copy-start
  7.2 0.0 all-gather.2.cloned.1.call-start
  7.2 0.7 all-gather.2.cloned.1.call-update
  7.9 0.0 all-reduce.2.cloned.1.call-start
  8.0 0.8 reshape.59
  8.8 0.8 reshape.57
  9.5 0.8 dynamic_slice.7
  10.3 0.0 copy-done
  10.3 59.0 %convolution_convert_fusion = bf16[16,12,3,256,256]{4,3,2,1,0:T(8,128)(2,1)} fusion(bf16[16,12,3,256,256]{4,3,2,1,0:T(8,128)(2,1)} %param.6, bf16[16,256,256,1,1]{2,1,4,3,0:T(8,128)(2,1)S(1)} %bitcast.20), kind=kOutput, calls=%fused_computation.1 | convolution fusion | flops 19365101568 | bytes 153092096 | tf_op jit(solution)/shard_map/rkast,rsu->rkatu/dot_general | solution.py:14
  69.4 70.4 %all-gather.2.cloned.1.call-done = bf16[65536,128]{1,0:T(8,128)(2,1)} async-done(((bf16[4096,128]{1,0:T(8,128)(2,1)}), bf16[65536,128]{1,0:T(8,128)(2,1)}) %all-gather.2.cloned.1.call-update) | async-done | bytes 16777232 | tf_op jit(solution)/shard_map/all_gather | solution.py:22
  139.8 13.9 %gather_fusion = bf16[192,256,128]{2,1,0:T(8,128)(2,1)} fusion(bf16[256,256,128]{2,1,0:T(8,128)(2,1)} %bitcast.21, s32[1024]{0:T(1024)S(1)} %pad_clamp_fusion), kind=kCustom, calls=%fused_computation | custom fusion | bytes 25166592 | tf_op jit(solution)/shard_map/jit(_take)/gather | solution.py:24
  153.7 0.0 copy-start.2
  153.8 32.8 %fusion.5 = f32[3,256,128]{2,1,0:T(8,128)} fusion(bf16[192,3,256,256]{3,2,1,0:T(8,128)(2,1)} %bitcast.3, bf16[192,256,128]{2,1,0:T(8,128)(2,1)} %gather_fusion, pred[192]{0:T(512)(128)(4,1)S(1)} %compare_and_fusion), kind=kOutput, calls=%fused_computation.7 | convolution fusion | flops 9669967872 | bytes 88473792 | tf_op jit(solution)/shard_map/eatu,etl->aul/dot_general | solution.py:25
  186.6 0.0 all-reduce.2.cloned.1.call-update
  186.6 0.0 copy-done.2
  186.6 88.6 %all-reduce.2.cloned.1.call-done = f32[3,256,128]{2,1,0:T(8,128)} async-done(((f32[3,256,128]{2,1,0:T(8,128)}), f32[3,256,128]{2,1,0:T(8,128)}) %all-reduce.2.cloned.1.call-update) | async-done | bytes 393232 | tf_op jit(solution)/shard_map/psum | solution.py:28
  275.2 0.7 multiply_reduce_fusion
  276.0 0.0 copy-start.1
  276.0 0.7 fusion.9
  276.7 0.0 copy-done.1
  (4 shorter events, 0.0 us)
Async XLA Ops:
  7.2 3.2 %copy-start = (bf16[4096,256]{1,0:T(8,128)(2,1)S(1)}, bf16[4096,256]{1,0:T(8,128)(2,1)}, u32[]{:S(2)}) copy-start(bf16[4096,256]{1,0:T(8,128)(2,1)} %param.8) | copy-start | bytes 6291460
  7.2 132.6 %all-gather.2.cloned.1.call-start = ((), (), s32[]{:S(2)}) async-start(), calls=%async_computation | async-start | bytes 17825792 | tf_op jit(solution)/shard_map/all_gather | solution.py:22
  7.9 267.3 %all-reduce.2.cloned.1.call-start = ((), (), s32[]{:S(2)}) async-start(), calls=%async_computation.1 | async-start | bytes 786432 | tf_op jit(solution)/shard_map/psum | solution.py:28
  153.7 32.8 %copy-start.2 = (f32[128]{0:T(128)S(1)}, f32[128]{0:T(128)}, u32[]{:S(2)}) copy-start(f32[128]{0:T(128)} %param.11) | copy-start | bytes 1540
  276.0 0.7 copy-start.1
Sparse Core Ops, SparseCore 0:
  10.2 129.5 all-gather.1
  186.7 88.4 all-reduce.1
where the time goes:
time: 284 us; the launch traced here: 283 us
  waiting for transfers between devices  160 us (56%)
  matrix products  91.9 us (32%)
  local copies, waits for them, and re-layouts  16.3 us (6%)
  between operations  14.1 us (5%)
    psum x1, waiting for transfers between devices, per_device(): summed = lax.psum(proj, 'blk')  88.6 us
    all_gather x1, waiting for transfers between devices, per_device(): gathered = lax.all_gather(lower_vecs, 'blk', axis=0, tiled=True)  70.4 us
    dot_general x1, matrix products, per_device(): jnp.einsum('rkast,rsu->rkatu', dipole, upper_blocks, preferred_element_ty...  59 us
    dot_general x1, matrix products, per_device(): jnp.einsum('eatu,etl->aul', halves, lows, preferred_element_type=jnp.floa...  32.8 us
    gather x1, local copies, waits for them, and re-layouts, per_device(): lows = jnp.take(all_blocks, columns, axis=0)  13.9 us
  transfers between devices with their start and end apart: 2, of which 2 were waited for; matrix products, arithmetic and copies ran while one was open for 22% of the time, Pallas kernels for 0%

commit v1 on v0

v1 whole, which is shorter than its diff:
```python
import functools

import jax
import jax.numpy as jnp
from jax import lax
from jax.experimental import pallas as pl
from jax.experimental.pallas import tpu as pltpu
from jax.sharding import PartitionSpec as P

THERMAL = 0.3
MESH = pl.DeviceIdType.MESH
LANES = 128
SLOTS = 13


def finish(own_share, energy_rows, lower_energy):
    strength = jnp.sum(own_share * own_share, axis=0)
    wavenumber = energy_rows - lower_energy
    intensity = wavenumber * wavenumber * wavenumber * jnp.exp(-lower_energy / THERMAL) * strength
    return strength, intensity


def plain_device(dipole, block_cols, upper_vecs, lower_vecs, upper_energy, lower_energy):
    rows_blk, nonzero, n_comps, block_size, _ = dipole.shape
    upper_count = upper_vecs.shape[1]
    lower_count = lower_vecs.shape[1]
    upper_blocks = upper_vecs.reshape(rows_blk, block_size, upper_count)
    halves = jnp.einsum(
        "rkast,rsu->rkatu", dipole, upper_blocks, preferred_element_type=jnp.float32
    ).astype(jnp.bfloat16)
    gathered = lax.all_gather(lower_vecs, "blk", axis=0, tiled=True)
    all_blocks = gathered.reshape(gathered.shape[0] // block_size, block_size, lower_count)
    lows = jnp.take(all_blocks, block_cols, axis=0)
    proj = jnp.einsum("rkatu,rktl->aul", halves, lows, preferred_element_type=jnp.float32)
    own_share = lax.psum_scatter(proj, "blk", scatter_dimension=1, tiled=True)
    share_rows = own_share.shape[1]
    first_row = lax.axis_index("blk") * share_rows
    energy_rows = lax.dynamic_slice_in_dim(upper_energy, first_row, share_rows, 0)
    return finish(own_share, energy_rows[:, None], lower_energy[None, :])


def kernel(
    grid, first_blocks,
    cols, upper_e, lower_e, d_hbm, u_hbm, l_hbm,
    strength_ref, intensity_ref,
    g0, g1, dbuf, ubuf, ut, proj, send_buf, core_in, core_sum, y_in, y_sum, z_in,
    recv_sem, send_sem, own_sem, d_sem, u_sem, red_send, red_recv,
):
    n_z, n_y = grid
    gathered = (g0, g1)
    rows, entries, block, _ = d_hbm.shape
    n_comps = proj.shape[0]
    nonzero = entries // n_comps
    me = lax.axis_index("blk")
    core = lax.rem(me, 2)
    y = lax.rem(me // 2, n_y)
    z = me // (2 * n_y)
    other_y = 1 - y

    def device(zz, yy, cc):
        return (zz * n_y + yy) * 2 + cc

    sibling = device(z, y, 1 - core)
    across = device(z, other_y, core)

    def d_copy(i):
        half, row = i // rows, lax.rem(i, rows)
        lanes = pl.ds(pl.multiple_of(half * LANES, LANES), LANES)
        slot = lax.rem(i, SLOTS)
        return pltpu.make_async_copy(d_hbm.at[row, :, :, lanes], dbuf.at[slot], d_sem.at[slot])

    u_copy = pltpu.make_async_copy(u_hbm, ubuf, u_sem)

    barrier = pltpu.get_barrier_semaphore()
    pl.semaphore_signal(barrier, inc=1, device_id={"blk": sibling}, device_id_type=MESH)
    pl.semaphore_signal(barrier, inc=1, device_id={"blk": across}, device_id_type=MESH)
    for off in range(1, n_z):
        pl.semaphore_signal(
            barrier, inc=1, device_id={"blk": device(lax.rem(z + off, n_z), y, core)}, device_id_type=MESH
        )
    own_copies = [
        pltpu.make_async_copy(l_hbm.at[:, h], gathered[h].at[pl.ds(me * rows, rows)], own_sem.at[h])
        for h in range(2)
    ]
    pl.semaphore_wait(barrier, n_z + 1)

    spans = ((0, first_blocks), (first_blocks, rows - first_blocks))
    DOWN, UP, CROSS, CORE = range(4)
    targets = (device(z - 1, y, core), device(z + 1, y, core), across, sibling)
    exists = (z > 0, z < n_z - 1, z >= 0, z >= 0)
    pending = []

    def block_copy(h, src, piece, way, own):
        start, size = spans[piece]
        here = gathered[h].at[pl.ds(src * rows + start, size)]
        return pltpu.make_async_remote_copy(
            src_ref=l_hbm.at[pl.ds(start, size), h] if own else here,
            dst_ref=here,
            send_sem=send_sem.at[h, way, src // 2, piece],
            recv_sem=recv_sem.at[h, src, piece],
            device_id={"blk": targets[way]},
            device_id_type=MESH,
        )

    def send(*where):
        @pl.when(exists[where[3]])
        def _():
            block_copy(*where).start()

    def arrived(h, src, piece):
        block_copy(h, src, piece, CORE, False).wait_recv()

    def pass_on(h, guard, src, piece, ways):
        pending.extend((guard, h, src, piece, way, False) for way in ways)

        @pl.when(guard)
        def _():
            arrived(h, src, piece)
            for way in ways:
                send(h, src, piece, way, False)

    def own_sends(h):
        for way, piece in (
            (CROSS, 1), (DOWN, 0), (UP, 0), (CROSS, 0), (DOWN, 1), (UP, 1), (CORE, 0), (CORE, 1)
        ):
            pending.append((z >= 0, h, me, piece, way, True))
            send(h, me, piece, way, True)

    def events(h):
        steps = [functools.partial(pass_on, h, z >= 0, across, 1, (DOWN, UP, CORE))]
        for off in range(1, n_z):
            low, high = z - off >= 0, z + off < n_z
            steps += [
                functools.partial(pass_on, h, low, device(z - off, y, core), 0, (UP, CROSS, CORE)),
                functools.partial(pass_on, h, high, device(z + off, y, core), 0, (DOWN, CROSS, CORE)),
            ]
            if off == 1:
                steps += [functools.partial(pass_on, h, z >= 0, across, 0, (CORE,))]
            else:
                steps += [
                    functools.partial(pass_on, h, z - off + 1 >= 0, device(z - off + 1, other_y, core), 0, (CORE,)),
                    functools.partial(pass_on, h, z + off - 1 < n_z, device(z + off - 1, other_y, core), 0, (CORE,)),
                ]
            for yy in (y, other_y):
                steps += [
                    functools.partial(pass_on, h, low, device(z - off, yy, core), 1, (UP, CORE)),
                    functools.partial(pass_on, h, high, device(z + off, yy, core), 1, (DOWN, CORE)),
                ]
        off = n_z - 1
        steps += [
            functools.partial(pass_on, h, z - off >= 0, device(z - off, other_y, core), 0, (CORE,)),
            functools.partial(pass_on, h, z + off < n_z, device(z + off, other_y, core), 0, (CORE,)),
        ]
        return steps

    def from_sibling(h):
        own_copies[h].wait()

        def one(i, carry):
            src = i * 2 + 1 - core
            arrived(h, src, 0)
            arrived(h, src, 1)
            return carry

        lax.fori_loop(0, n_z * n_y, one, 0)

    def products(h, lo, hi):
        def one_row(r, carry):
            i = h * rows + r
            d_copy(i).wait()
            slot = lax.rem(i, SLOTS)

            def one_comp(a, inner):
                total = None
                for k in range(0, nonzero, 2):
                    left = jnp.concatenate(
                        [dbuf[slot, k * n_comps + a], dbuf[slot, (k + 1) * n_comps + a]], axis=1
                    )
                    right = jnp.concatenate(
                        [gathered[h][cols[r * nonzero + k]], gathered[h][cols[r * nonzero + k + 1]]], axis=0
                    )
                    term = jnp.dot(left, right, preferred_element_type=jnp.float32)
                    total = term if total is None else total + term
                high = total.astype(jnp.bfloat16)
                low = (total - high.astype(jnp.float32)).astype(jnp.bfloat16)
                both = jnp.dot(
                    ut[r], jnp.concatenate([high, low], axis=1), preferred_element_type=jnp.float32
                )
                proj[a] += both[:, :LANES] + both[:, LANES:]
                return inner

            lax.fori_loop(0, n_comps, one_comp, 0)

            @pl.when(i + SLOTS < 2 * rows)
            def _():
                d_copy(i + SLOTS).start()

            return carry

        lax.fori_loop(lo, hi, one_row, 0)

    own_sends(0)
    u_copy.start()
    own_copies[0].start()
    own_copies[1].start()

    def prefetch(i, carry):
        d_copy(i).start()
        return carry

    lax.fori_loop(0, min(SLOTS, 2 * rows), prefetch, 0)
    proj[...] = jnp.zeros_like(proj)
    u_copy.wait()

    def turn(r, carry):
        ut[r] = ubuf[r].astype(jnp.float32).T.astype(jnp.bfloat16)
        return carry

    lax.fori_loop(0, rows, turn, 0)

    for step in events(0):
        step()
    own_sends(1)
    from_sibling(0)
    steps = events(1)
    chunks = min(8, rows)
    done = 0
    for n, step in enumerate(steps):
        step()
        goal = (n + 1) * chunks // len(steps)
        if goal > done:
            products(0, done * rows // chunks, goal * rows // chunks)
            done = goal
    from_sibling(1)
    products(1, 0, rows)

    n_dev = 2 * n_y * n_z
    share = strength_ref.shape[0]
    for i in range(n_dev):
        send_buf[i // 2, i % 2] = proj[:, i * share:(i + 1) * share, :]

    def reduce_copy(src, dst, slot, target):
        return pltpu.make_async_remote_copy(
            src_ref=src, dst_ref=dst, send_sem=red_send.at[slot], recv_sem=red_recv.at[slot],
            device_id={"blk": target}, device_id_type=MESH,
        )

    copy = reduce_copy(send_buf.at[:, 1 - core], core_in, 0, sibling)
    copy.start()
    copy.wait()
    for i in range(n_z * n_y):
        core_sum[i % n_y, i // n_y] = send_buf[i, core] + core_in[i]
    copy = reduce_copy(core_sum.at[other_y], y_in, 1, across)
    copy.start()
    copy.wait()
    y_sum[...] = core_sum[y] + y_in[...]
    copies = []
    for off in range(1, n_z):
        to = lax.rem(z + off, n_z)
        copy = reduce_copy(y_sum.at[to], z_in.at[off - 1], 1 + off, device(to, y, core))
        copy.start()
        copies.append(copy)
    total = y_sum[z]
    for off, copy in enumerate(copies):
        copy.wait()
        total = total + z_in[off]

    places = lax.broadcasted_iota(jnp.int32, (share, LANES), 0)
    energy_rows = jnp.zeros((share, LANES), jnp.float32)
    for j in range(share):
        energy_rows = jnp.where(places == j, upper_e[me * share + j], energy_rows)
    strength_ref[...], intensity_ref[...] = finish(total, energy_rows, lower_e[...])

    for guard, *where in pending:
        @pl.when(jnp.logical_and(guard, exists[where[3]]))
        def _():
            block_copy(*where).wait_send()


def kernel_device(grid, dipole, block_cols, upper_vecs, lower_vecs, upper_energy, lower_energy):
    rows, nonzero, n_comps, block, _ = dipole.shape
    upper_count = upper_vecs.shape[1]
    lower_count = lower_vecs.shape[1]
    n_z, n_y = grid
    n_dev = 2 * n_y * n_z
    share = upper_count // n_dev
    balance = (n_z * n_y - 2 * n_y + 1) / (2 * (n_z - 1) * (n_y - 1))
    first_blocks = min(rows - 1, max(1, round(rows * balance)))
    f32, bf16 = jnp.float32, jnp.bfloat16
    out = jax.ShapeDtypeStruct((share, lower_count), f32)
    dma = pltpu.SemaphoreType.DMA
    return tuple(pl.pallas_call(
        functools.partial(kernel, grid, first_blocks),
        out_shape=(out, out),
        in_specs=[
            pl.BlockSpec(memory_space=pltpu.SMEM),
            pl.BlockSpec(memory_space=pltpu.SMEM),
            pl.BlockSpec(memory_space=pltpu.VMEM),
            pl.BlockSpec(memory_space=pl.ANY),
            pl.BlockSpec(memory_space=pl.ANY),
            pl.BlockSpec(memory_space=pl.ANY),
        ],
        out_specs=(pl.BlockSpec(memory_space=pltpu.VMEM), pl.BlockSpec(memory_space=pltpu.VMEM)),
        scratch_shapes=[
            pltpu.VMEM((n_dev * rows, block // 2, lower_count), bf16),
            pltpu.VMEM((n_dev * rows, block // 2, lower_count), bf16),
            pltpu.VMEM((SLOTS, nonzero * n_comps, block, block // 2), bf16),
            pltpu.VMEM((rows, block, upper_count), bf16),
            pltpu.VMEM((rows, upper_count, block), bf16),
            pltpu.VMEM((n_comps, upper_count, lower_count), f32),
            pltpu.VMEM((n_z * n_y, 2, n_comps, share, lower_count), f32),
            pltpu.VMEM((n_z * n_y, n_comps, share, lower_count), f32),
            pltpu.VMEM((n_y, n_z, n_comps, share, lower_count), f32),
            pltpu.VMEM((n_z, n_comps, share, lower_count), f32),
            pltpu.VMEM((n_z, n_comps, share, lower_count), f32),
            pltpu.VMEM((n_z - 1, n_comps, share, lower_count), f32),
            dma((2, n_dev, 2)),
            dma((2, 4, n_dev // 2, 2)),
            dma((2,)),
            dma((SLOTS,)),
            dma,
            dma((n_z + 1,)),
            dma((n_z + 1,)),
        ],
        compiler_params=pltpu.CompilerParams(
            collective_id=0, has_side_effects=True, vmem_limit_bytes=60 << 20
        ),
    )(
        block_cols.reshape(-1),
        upper_energy,
        lower_energy.reshape(1, lower_count),
        dipole.reshape(rows, nonzero * n_comps, block, block),
        upper_vecs.reshape(rows, block, upper_count),
        lower_vecs.reshape(rows, 2, block // 2, lower_count),
    ))


def solution(mesh):
    grid = {16: (4, 2)}.get(mesh.shape["blk"])
    per_device = functools.partial(kernel_device, grid) if grid else plain_device
    placed = (
        P("blk", None, None, None, None),
        P("blk", None),
        P(("jpair", "blk"), None),
        P(("jpair", "blk"), None),
        P("jpair"),
        P("jpair"),
    )
    return jax.shard_map(
        per_device,
        mesh=mesh,
        in_specs=placed,
        out_specs=(P(("jpair", "blk"), None), P(("jpair", "blk"), None)),
        check_vma=False,
    )
```

time: 284 us -> 144 us (0.51)
  waiting for transfers between devices: 160 us -> 0 us
  Pallas kernels: 0 us -> 139 us
  matrix products: 91.9 us -> 0 us
  between operations: 14.1 us -> 0.64 us
  local copies, waits for them, and re-layouts: 16.3 us -> 3.94 us
    pallas_call x0 -> x1, Pallas kernels: none -> 139 us  [kernel_device(): pl.pallas_call(functools.partial(kernel, grid, first_blocks), out_shape=(...]
    dot_general x2 -> x0, matrix products: 91.9 us -> none  [the longest x1 59 us: per_device(): jnp.einsum('rkast,rsu->rkatu', dipole, upper_blocks, preferred_element_ty...]
    psum x1 -> x0, waiting for transfers between devices: 88.6 us -> none  [per_device(): summed = lax.psum(proj, 'blk')]
    all_gather x1 -> x0, waiting for transfers between devices: 70.4 us -> none  [per_device(): gathered = lax.all_gather(lower_vecs, 'blk', axis=0, tiled=True)]
    gather x1 -> x0, local copies, waits for them, and re-layouts: 13.9 us -> none  [per_device(): lows = jnp.take(all_blocks, columns, axis=0)]
  transfers between devices with their start and end apart: 2 -> 0, of which waited for: 2 -> 0; matrix products, arithmetic and copies ran while one was open for 22% -> 0% of each run, Pallas kernels for 0% -> 0%
where the time goes in v1:
time: 144 us; the launch traced here: 143 us
  Pallas kernels  139 us (97%)
  local copies, waits for them, and re-layouts  3.94 us (3%)
    pallas_call x1, Pallas kernels, kernel_device(): pl.pallas_call(functools.partial(kernel, grid, first_blocks), out_shape=(...  139 us

profile of v1, /device:TPU:0, one launch (start us, length us, event | category | flops | bytes accessed | tf_op | source)
XLA Modules:
  0.0 143.3 jit_solution(12784195802312704281)
XLA Ops:
  0.6 1.3 reshape.19.cols
  2.0 138.8 %shard_map.77 = (f32[16,128]{1,0:T(8,128)}, f32[16,128]{1,0:T(8,128)}) custom-call(s32[192]{0:T(256)} %reshape.19.cols, f32[256]{0:T(256)} %upper_e.1, f32[1,128]{1,0:T(1,128)} %bitcast.6, bf16[16,36,256,256]{3,2,1,0:T(8,128)(2,1)} %bitcast.1.d_hbm, bf16[16,256,256]{2,1,0:T(8,128)(2,1)} %bitcast.4, bf16[16,2,128,128]{3,2,1,0:T(8,128)(2,1)} %bitcast.5), custom_call_target="tpu_custom_call" | custom-call | tf_op jit(solution)/shard_map/pallas_call | solution.py:292
  140.8 1.3 copy.10
  142.0 1.3 copy.11

commit v2 on v1

--- a/solution.py
+++ b/solution.py
@@ -10,7 +10,8 @@
 THERMAL = 0.3
 MESH = pl.DeviceIdType.MESH
 LANES = 128
-SLOTS = 13
+SLOTS = 36
+UNROLL = 4
 
 
 def finish(own_share, energy_rows, lower_energy):
@@ -41,16 +42,15 @@
 
 def kernel(
     grid, first_blocks,
-    cols, upper_e, lower_e, d_hbm, u_hbm, l_hbm,
-    strength_ref, intensity_ref,
-    g0, g1, dbuf, ubuf, ut, proj, send_buf, core_in, core_sum, y_in, y_sum, z_in,
+    cols, d_hbm, u_hbm, l_hbm,
+    own_ref,
+    g0, g1, dbuf, ubuf, ut, sums, split, send_buf, core_in, core_sum, y_in, y_sum, z_in,
     recv_sem, send_sem, own_sem, d_sem, u_sem, red_send, red_recv,
 ):
     n_z, n_y = grid
     gathered = (g0, g1)
-    rows, entries, block, _ = d_hbm.shape
-    n_comps = proj.shape[0]
-    nonzero = entries // n_comps
+    rows, nonzero, n_comps, block, _ = d_hbm.shape
+    units = n_comps * rows
     me = lax.axis_index("blk")
     core = lax.rem(me, 2)
     y = lax.rem(me // 2, n_y)
@@ -64,10 +64,10 @@
     across = device(z, other_y, core)
 
     def d_copy(i):
-        half, row = i // rows, lax.rem(i, rows)
+        half, comp, row = i // units, lax.rem(i, units) // rows, lax.rem(i, rows)
         lanes = pl.ds(pl.multiple_of(half * LANES, LANES), LANES)
         slot = lax.rem(i, SLOTS)
-        return pltpu.make_async_copy(d_hbm.at[row, :, :, lanes], dbuf.at[slot], d_sem.at[slot])
+        return pltpu.make_async_copy(d_hbm.at[row, :, comp, :, lanes], dbuf.at[slot], d_sem.at[slot])
 
     u_copy = pltpu.make_async_copy(u_hbm, ubuf, u_sem)
 
@@ -165,39 +165,80 @@
         lax.fori_loop(0, n_z * n_y, one, 0)
 
     def products(h, lo, hi):
-        def one_row(r, carry):
-            i = h * rows + r
-            d_copy(i).wait()
-            slot = lax.rem(i, SLOTS)
-
-            def one_comp(a, inner):
-                total = None
-                for k in range(0, nonzero, 2):
-                    left = jnp.concatenate(
-                        [dbuf[slot, k * n_comps + a], dbuf[slot, (k + 1) * n_comps + a]], axis=1
-                    )
-                    right = jnp.concatenate(
-                        [gathered[h][cols[r * nonzero + k]], gathered[h][cols[r * nonzero + k + 1]]], axis=0
-                    )
-                    term = jnp.dot(left, right, preferred_element_type=jnp.float32)
-                    total = term if total is None else total + term
-                high = total.astype(jnp.bfloat16)
-                low = (total - high.astype(jnp.float32)).astype(jnp.bfloat16)
-                both = jnp.dot(
-                    ut[r], jnp.concatenate([high, low], axis=1), preferred_element_type=jnp.float32
-                )
-                proj[a] += both[:, :LANES] + both[:, LANES:]
-                return inner
-
-            lax.fori_loop(0, n_comps, one_comp, 0)
-
-            @pl.when(i + SLOTS < 2 * rows)
-            def _():
-                d_copy(i + SLOTS).start()
+        def some_units(n, carry):
+            first = lo + n * UNROLL
+            for j in range(UNROLL):
+                d_copy(h * units + first + j).wait()
+            for j in range(UNROLL):
+                unit = first + j
+                slot = lax.rem(h * units + unit, SLOTS)
+                row = lax.rem(unit, rows)
+                left = jnp.concatenate([dbuf[slot, k] for k in range(nonzero)], axis=1)
+                right = jnp.concatenate([gathered[h][cols[row, k]] for k in range(nonzero)], axis=0)
+                total = jnp.dot(left, right, preferred_element_type=jnp.float32)
+                if h == 0:
+                    sums[unit] = total
+                else:
+                    total = total + sums[unit]
+                    high = total.astype(jnp.bfloat16)
+                    low = (total - high.astype(jnp.float32)).astype(jnp.bfloat16)
+                    split[row, :, :LANES] = high
+                    split[row, :, LANES:] = low
+            for j in range(UNROLL):
+                later = h * units + first + j + SLOTS
+
+                @pl.when(later < 2 * units)
+                def _():
+                    d_copy(later).start()
 
             return carry
 
-        lax.fori_loop(lo, hi, one_row, 0)
+        lax.fori_loop(0, (hi - lo) // UNROLL, some_units, 0)
+
+    n_dev = 2 * n_y * n_z
+    share = own_ref.shape[1]
+
+    def reduce_copy(a, src, dst, slot, target):
+        return pltpu.make_async_remote_copy(
+            src_ref=src, dst_ref=dst, send_sem=red_send.at[a, slot], recv_sem=red_recv.at[a, slot],
+            device_id={"blk": target}, device_id_type=MESH,
+        )
+
+    def over_core(a):
+        return reduce_copy(a, send_buf.at[a, :, 1 - core], core_in.at[a], 0, sibling)
+
+    def over_y(a):
+        return reduce_copy(a, core_sum.at[a, other_y], y_in.at[a], 1, across)
+
+    def over_z(a, off):
+        to = lax.rem(z + off, n_z)
+        return reduce_copy(a, y_sum.at[a, to], z_in.at[a, off - 1], 1 + off, device(to, y, core))
+
+    def start_core(a):
+        both = jnp.dot(ut[...], split[...].reshape(rows * block, 2 * LANES), preferred_element_type=jnp.float32)
+        part = both[:, :LANES] + both[:, LANES:]
+        for i in range(n_dev):
+            send_buf[a, i // 2, i % 2] = part[i * share:(i + 1) * share]
+        over_core(a).start()
+
+    def start_y(a):
+        over_core(a).wait()
+        for i in range(n_z * n_y):
+            core_sum[a, i % n_y, i // n_y] = send_buf[a, i, core] + core_in[a, i]
+        over_y(a).start()
+
+    def start_z(a):
+        over_y(a).wait()
+        y_sum[a] = core_sum[a, y] + y_in[a]
+        for off in range(1, n_z):
+            over_z(a, off).start()
+
+    def close(a):
+        total = y_sum[a, z]
+        for off in range(1, n_z):
+            over_z(a, off).wait()
+            total = total + z_in[a, off - 1]
+        own_ref[a] = total
 
     own_sends(0)
     u_copy.start()
@@ -208,12 +249,12 @@
         d_copy(i).start()
         return carry
 
-    lax.fori_loop(0, min(SLOTS, 2 * rows), prefetch, 0)
-    proj[...] = jnp.zeros_like(proj)
+    lax.fori_loop(0, min(SLOTS, 2 * units), prefetch, 0)
     u_copy.wait()
 
     def turn(r, carry):
-        ut[r] = ubuf[r].astype(jnp.float32).T.astype(jnp.bfloat16)
+        lanes = pl.ds(pl.multiple_of(r * block, block), block)
+        ut[:, lanes] = ubuf[r].astype(jnp.float32).T.astype(jnp.bfloat16)
         return carry
 
     lax.fori_loop(0, rows, turn, 0)
@@ -223,53 +264,28 @@
     own_sends(1)
     from_sibling(0)
     steps = events(1)
-    chunks = min(8, rows)
+    chunks = units // UNROLL
     done = 0
     for n, step in enumerate(steps):
         step()
         goal = (n + 1) * chunks // len(steps)
         if goal > done:
-            products(0, done * rows // chunks, goal * rows // chunks)
+            products(0, done * UNROLL, goal * UNROLL)
             done = goal
     from_sibling(1)
-    products(1, 0, rows)
-
-    n_dev = 2 * n_y * n_z
-    share = strength_ref.shape[0]
-    for i in range(n_dev):
-        send_buf[i // 2, i % 2] = proj[:, i * share:(i + 1) * share, :]
-
-    def reduce_copy(src, dst, slot, target):
-        return pltpu.make_async_remote_copy(
-            src_ref=src, dst_ref=dst, send_sem=red_send.at[slot], recv_sem=red_recv.at[slot],
-            device_id={"blk": target}, device_id_type=MESH,
-        )
-
-    copy = reduce_copy(send_buf.at[:, 1 - core], core_in, 0, sibling)
-    copy.start()
-    copy.wait()
-    for i in range(n_z * n_y):
-        core_sum[i % n_y, i // n_y] = send_buf[i, core] + core_in[i]
-    copy = reduce_copy(core_sum.at[other_y], y_in, 1, across)
-    copy.start()
-    copy.wait()
-    y_sum[...] = core_sum[y] + y_in[...]
-    copies = []
-    for off in range(1, n_z):
-        to = lax.rem(z + off, n_z)
-        copy = reduce_copy(y_sum.at[to], z_in.at[off - 1], 1 + off, device(to, y, core))
-        copy.start()
-        copies.append(copy)
-    total = y_sum[z]
-    for off, copy in enumerate(copies):
-        copy.wait()
-        total = total + z_in[off]
-
-    places = lax.broadcasted_iota(jnp.int32, (share, LANES), 0)
-    energy_rows = jnp.zeros((share, LANES), jnp.float32)
-    for j in range(share):
-        energy_rows = jnp.where(places == j, upper_e[me * share + j], energy_rows)
-    strength_ref[...], intensity_ref[...] = finish(total, energy_rows, lower_e[...])
+    half = rows // 2
+    for a in range(n_comps):
+        products(1, a * rows, a * rows + half)
+        if a > 0:
+            start_y(a - 1)
+        products(1, a * rows + half, (a + 1) * rows)
+        if a > 0:
+            start_z(a - 1)
+        start_core(a)
+    start_y(n_comps - 1)
+    start_z(n_comps - 1)
+    for a in range(n_comps):
+        close(a)
 
     for guard, *where in pending:
         @pl.when(jnp.logical_and(guard, exists[where[3]]))
@@ -287,52 +303,50 @@
     balance = (n_z * n_y - 2 * n_y + 1) / (2 * (n_z - 1) * (n_y - 1))
     first_blocks = min(rows - 1, max(1, round(rows * balance)))
     f32, bf16 = jnp.float32, jnp.bfloat16
-    out = jax.ShapeDtypeStruct((share, lower_count), f32)
     dma = pltpu.SemaphoreType.DMA
-    return tuple(pl.pallas_call(
+    own_share = pl.pallas_call(
         functools.partial(kernel, grid, first_blocks),
-        out_shape=(out, out),
+        out_shape=jax.ShapeDtypeStruct((n_comps, share, lower_count), f32),
         in_specs=[
             pl.BlockSpec(memory_space=pltpu.SMEM),
-            pl.BlockSpec(memory_space=pltpu.SMEM),
-            pl.BlockSpec(memory_space=pltpu.VMEM),
             pl.BlockSpec(memory_space=pl.ANY),
             pl.BlockSpec(memory_space=pl.ANY),
             pl.BlockSpec(memory_space=pl.ANY),
         ],
-        out_specs=(pl.BlockSpec(memory_space=pltpu.VMEM), pl.BlockSpec(memory_space=pltpu.VMEM)),
+        out_specs=pl.BlockSpec(memory_space=pltpu.VMEM),
         scratch_shapes=[
             pltpu.VMEM((n_dev * rows, block // 2, lower_count), bf16),
             pltpu.VMEM((n_dev * rows, block // 2, lower_count), bf16),
-            pltpu.VMEM((SLOTS, nonzero * n_comps, block, block // 2), bf16),
+            pltpu.VMEM((SLOTS, nonzero, block, block // 2), bf16),
             pltpu.VMEM((rows, block, upper_count), bf16),
-            pltpu.VMEM((rows, upper_count, block), bf16),
-            pltpu.VMEM((n_comps, upper_count, lower_count), f32),
-            pltpu.VMEM((n_z * n_y, 2, n_comps, share, lower_count), f32),
-            pltpu.VMEM((n_z * n_y, n_comps, share, lower_count), f32),
-            pltpu.VMEM((n_y, n_z, n_comps, share, lower_count), f32),
-            pltpu.VMEM((n_z, n_comps, share, lower_count), f32),
-            pltpu.VMEM((n_z, n_comps, share, lower_count), f32),
-            pltpu.VMEM((n_z - 1, n_comps, share, lower_count), f32),
+            pltpu.VMEM((upper_count, rows * block), bf16),
+            pltpu.VMEM((n_comps * rows, block, lower_count), f32),
+            pltpu.VMEM((rows, block, 2 * lower_count), bf16),
+            pltpu.VMEM((n_comps, n_z * n_y, 2, share, lower_count), f32),
+            pltpu.VMEM((n_comps, n_z * n_y, share, lower_count), f32),
+            pltpu.VMEM((n_comps, n_y, n_z, share, lower_count), f32),
+            pltpu.VMEM((n_comps, n_z, share, lower_count), f32),
+            pltpu.VMEM((n_comps, n_z, share, lower_count), f32),
+            pltpu.VMEM((n_comps, n_z - 1, share, lower_count), f32),
             dma((2, n_dev, 2)),
             dma((2, 4, n_dev // 2, 2)),
             dma((2,)),
             dma((SLOTS,)),
             dma,
-            dma((n_z + 1,)),
-            dma((n_z + 1,)),
+            dma((n_comps, n_z + 1)),
+            dma((n_comps, n_z + 1)),
         ],
         compiler_params=pltpu.CompilerParams(
-            collective_id=0, has_side_effects=True, vmem_limit_bytes=60 << 20
+            collective_id=0, has_side_effects=True, vmem_limit_bytes=62 << 20
         ),
     )(
-        block_cols.reshape(-1),
-        upper_energy,
-        lower_energy.reshape(1, lower_count),
-        dipole.reshape(rows, nonzero * n_comps, block, block),
+        block_cols,
+        dipole,
         upper_vecs.reshape(rows, block, upper_count),
         lower_vecs.reshape(rows, 2, block // 2, lower_count),
-    ))
+    )
+    energy_rows = lax.dynamic_slice_in_dim(upper_energy, lax.axis_index("blk") * share, share, 0)
+    return finish(own_share, energy_rows[:, None], lower_energy[None, :])
 
 
 def solution(mesh):

time: 144 us -> 124 us (0.86)
  Pallas kernels: 139 us -> 121 us
  local copies, waits for them, and re-layouts: 3.94 us -> 0.09 us
    pallas_call x1, Pallas kernels: 139 us -> 121 us  [kernel_device(): pl.pallas_call(functools.partial(kernel, grid, first_blocks), out_shape=j...]
    unnamed x2 -> x6, local copies, waits for them, and re-layouts: 2.59 us -> 0.01 us
where the time goes in v2:
time: 124 us; the launch traced here: 123 us
  Pallas kernels  121 us (98%)
  other arithmetic  1.43 us (1%)
    pallas_call x1, Pallas kernels, kernel_device(): pl.pallas_call(functools.partial(kernel, grid, first_blocks), out_shape=j...  121 us

profile of v2, /device:TPU:0, one launch (start us, length us, event | category | flops | bytes accessed | tf_op | source)
XLA Modules:
  0.0 123.3 jit_solution(1255319458025894720)
XLA Ops:
  0.6 0.0 copy-start.1
  0.6 0.0 copy-start.2
  0.7 121.1 %shard_map.77 = f32[3,16,128]{2,1,0:T(8,128)} custom-call(s32[16,12]{1,0:T(8,128)} %cols.1, bf16[16,12,3,256,256]{4,3,2,1,0:T(8,128)(2,1)} %d_hbm.1, bf16[16,256,256]{2,1,0:T(8,128)(2,1)} %bitcast.2, bf16[16,2,128,128]{3,2,1,0:T(8,128)(2,1)} %bitcast.3), custom_call_target="tpu_custom_call" | custom-call | tf_op jit(solution)/shard_map/pallas_call | solution.py:307
  121.7 0.7 multiply_reduce_fusion
  122.5 0.0 copy-done.1
  122.5 0.0 copy-start
  122.5 0.0 copy-done.2
  122.5 0.1 dynamic_slice.3
  122.6 0.7 fusion.1
  123.3 0.0 copy-done
  (1 shorter events, 0.0 us)
Async XLA Ops:
  0.6 121.9 %copy-start.1 = (f32[128]{0:T(128)S(1)}, f32[128]{0:T(128)}, u32[]{:S(2)}) copy-start(f32[128]{0:T(128)} %param.11) | copy-start | bytes 1540
  0.6 121.9 %copy-start.2 = (f32[256]{0:T(256)S(1)}, f32[256]{0:T(256)}, u32[]{:S(2)}) copy-start(f32[256]{0:T(256)} %param.10) | copy-start | bytes 3076
  122.5 0.8 copy-start
